TPU v7x, 32 devices: a whole 2x2x4 slice. The times are simulated.
32 devices in a mesh: ctx: 8 (over z, x), head: 4 (over y, core).
Axes of the slice: x: 2, y: 2, z: 4, core: 2. Of those that a mesh axis runs over, the one named last changes fastest.
Arguments:
- token_keys: bfloat16 [8, 2048, 128], P(None, ('ctx', 'head')), may hold values from -4.5 to 4.5
- token_values: bfloat16 [8, 2048, 128], P(None, ('ctx', 'head')), may hold values from -6 to 6
- queries: bfloat16 [8, 2048, 8, 128], P(None, ('ctx', 'head')), may hold values from -16 to 16
- out_grad: bfloat16 [8, 2048, 8, 128], P(None, ('ctx', 'head')), may hold values from -6 to 6
- slot_ids: int32 [8, 2048], P('head'), may hold values from 0 to 511, as said below
Outputs:
- attended: bfloat16 [8, 2048, 8, 128], P(None, ('ctx', 'head'))
- key_grad: float32 [8, 2048, 128], P(None, ('ctx', 'head'))
- value_grad: float32 [8, 2048, 128], P(None, ('ctx', 'head'))
Inputs may be any that keep to these rules, and one draw needn't show every extreme that they name: `slot_ids`: in each head's row slot numbers never fall; each of the 512 slots holds 1 to 16 consecutive tokens; slots k * 64 to (k + 1) * 64 - 1 all begin among tokens k * 256 to (k + 1) * 256 - 1; every such block of tokens holds a slot of exactly 16 tokens.
All inputs are finite; a program needn't handle non-finite values.
Results may differ from a plain program's by a relative error of at most 0.012.
The roundings to bfloat16 on the way count: a program that leaves them out, or rounds other values in their place, can miss the bound.
Values may be sent and summed in bfloat16 or wider, within the bound.
A program may use at most 64 MiB of HBM per device.

v0:
```python
import math

import jax
import jax.numpy as jnp
from jax import lax
from jax.sharding import PartitionSpec as P

RATIO = 4


neg_big = -1e30


def from_behind(value, axis, steps):
    count = lax.axis_size(axis)
    initial, last = (max(0, -steps), min(count, count - steps))
    return lax.ppermute(value, axis, [(source, source + steps) for source in range(initial, last)])


def one_hot_rows(own_ids, first_row, how_many):
    relative = own_ids - first_row
    columns = jnp.arange(how_many, dtype=jnp.int32)
    return (relative[:, :, None] == columns[None, None, :]).astype(jnp.bfloat16)


def per_device(token_keys, token_values, queries, out_grad, slot_ids):
    keys_here, values_here, query_here, grad_here = (
        lax.all_to_all(token_keys, "head", split_axis=0, concat_axis=1, tiled=True),
        lax.all_to_all(token_values, "head", split_axis=0, concat_axis=1, tiled=True),
        lax.all_to_all(queries, "head", split_axis=0, concat_axis=1, tiled=True),
        lax.all_to_all(out_grad, "head", split_axis=0, concat_axis=1, tiled=True),
    )
    local_heads, tok_count, head_dim = keys_here.shape
    query_count = query_here.shape[1]
    group_size = query_here.shape[2]
    slot_count = tok_count // RATIO
    id_heads, context_len = slot_ids.shape
    total_slots = context_len // RATIO
    block_count = context_len // tok_count
    ctx_index = lax.axis_index("ctx")
    blocked_ids = slot_ids.reshape(id_heads, block_count, tok_count)
    block_base = jnp.arange(block_count, dtype=jnp.int32)
    targets = block_base[:, None] * slot_count + jnp.arange(slot_count, dtype=jnp.int32)[None, :]
    below_count = jnp.sum(
        (blocked_ids[:, :, :, None] < targets[None, :, None, :]).astype(jnp.int32), axis=2
    )
    starts_all = (block_base[None, :, None] * tok_count + below_count).reshape(
        id_heads, total_slots
    )
    slot_edges = jnp.concatenate(
        [starts_all, jnp.full((id_heads, 1), context_len, jnp.int32)], axis=1
    )
    slot_start = starts_all.T
    slot_len = slot_edges[:, 1:] - slot_edges[:, :-1]
    lengths_t = slot_len.T.astype(jnp.float32)[:, :, None]
    own_ids = lax.dynamic_slice_in_dim(slot_ids, ctx_index * tok_count, tok_count, 1)
    pair_low = jnp.concatenate([keys_here, values_here], axis=2)
    first_slot = ctx_index * slot_count - 1
    hot = one_hot_rows(own_ids, first_slot, slot_count + 1)
    window = jnp.einsum("htn,htc->nhc", hot, pair_low, preferred_element_type=jnp.float32)
    carried = from_behind(window[:1], "ctx", -1)
    padding = jnp.zeros((slot_count - 1, local_heads, 2 * head_dim), jnp.float32)
    own_sums = window[1:] + jnp.concatenate([padding, carried], axis=0)
    own_len = lax.dynamic_slice_in_dim(lengths_t, ctx_index * slot_count, slot_count, 0)
    slot_pairs = (own_sums / own_len).astype(jnp.bfloat16)
    rows_here = query_count * group_size
    query_rows = query_here.reshape(local_heads, rows_here, head_dim)
    grad_rows = grad_here.reshape(local_heads, rows_here, head_dim)
    stride = tok_count // query_count
    positions = jnp.repeat(
        (ctx_index * query_count + jnp.arange(query_count, dtype=jnp.int32)) * stride + stride - 1,
        group_size,
    )
    last_position = (ctx_index + 1) * query_count * stride - 1
    score_scale = 1.0 / math.sqrt(head_dim)

    def block_scores(key_block):
        scores = (
            jnp.einsum("hrd,nhd->hrn", query_rows, key_block, preferred_element_type=jnp.float32)
            * score_scale
        )
        visible = slot_start.T[:, None, :] <= positions[None, :, None]
        return (scores, visible)

    def reaches(first_row):
        return (
            jnp.min(lax.dynamic_index_in_dim(slot_start, first_row, 0, keepdims=False))
            <= last_position
        )

    init_stats = (
        jnp.full((local_heads, rows_here), neg_big, jnp.float32),
        jnp.zeros((local_heads, rows_here), jnp.float32),
    )
    key_block = lax.all_gather(slot_pairs[:, :, :head_dim], "ctx", axis=0, tiled=True)

    def stats_advance(state_in):
        top_now, mass_now = state_in
        scores, visible = block_scores(key_block)
        top_new = jnp.maximum(top_now, jnp.max(jnp.where(visible, scores, neg_big), axis=2))
        fresh = jnp.sum(jnp.where(visible, jnp.exp(scores - top_new[:, :, None]), 0.0), axis=2)
        return (top_new, fresh)

    row_top, row_mass = lax.cond(
        reaches(jnp.int32(0)), stats_advance, lambda state_in: state_in, init_stats
    )
    log_total = row_top + jnp.log(row_mass)

    def weights_of(pair_block):
        scores, visible = block_scores(pair_block[:, :, :head_dim])
        return jnp.where(visible, jnp.exp(scores - log_total[:, :, None]), 0.0)

    init_acc = jnp.zeros((local_heads, rows_here, head_dim), jnp.float32)
    pair_block = lax.all_gather(slot_pairs, "ctx", axis=0, tiled=True)

    def value_advance(state_in):
        weights_low = weights_of(pair_block).astype(jnp.bfloat16)
        return jnp.einsum(
            "hrn,nhd->hrd",
            weights_low,
            pair_block[:, :, head_dim:],
            preferred_element_type=jnp.float32,
        )

    summed_out = lax.cond(reaches(jnp.int32(0)), value_advance, lambda state_in: state_in, init_acc)
    attended = summed_out.astype(jnp.bfloat16)
    out_back = lax.all_to_all(
        attended.reshape(local_heads, query_count, group_size, head_dim),
        "head",
        split_axis=1,
        concat_axis=0,
        tiled=True,
    )
    row_dot = jnp.sum(grad_rows.astype(jnp.float32) * attended.astype(jnp.float32), axis=2)
    init_partials = jnp.zeros((total_slots, local_heads, 2 * head_dim), jnp.float32)
    grad_pair_block = lax.all_gather(slot_pairs, "ctx", axis=0, tiled=True)

    def grad_advance(state_in):
        weights = weights_of(grad_pair_block)
        weights_low = weights.astype(jnp.bfloat16)
        value_grads = jnp.einsum(
            "hrn,hrd->nhd", weights_low, grad_rows, preferred_element_type=jnp.float32
        )
        weight_grads = jnp.einsum(
            "hrd,nhd->hrn",
            grad_rows,
            grad_pair_block[:, :, head_dim:],
            preferred_element_type=jnp.float32,
        )
        dscores = (weights * (weight_grads - row_dot[:, :, None])).astype(jnp.bfloat16)
        key_grads = (
            jnp.einsum("hrn,hrd->nhd", dscores, query_rows, preferred_element_type=jnp.float32)
            * score_scale
        )
        return jnp.concatenate([key_grads, value_grads], axis=2)

    partials = lax.cond(
        reaches(jnp.int32(0)), grad_advance, lambda state_in: state_in, init_partials
    )
    share_grads = lax.psum_scatter(
        partials.astype(jnp.bfloat16), "ctx", scatter_dimension=0, tiled=True
    )
    below_row = from_behind(share_grads[-1:], "ctx", 1)
    grad_window = jnp.concatenate([below_row, share_grads], axis=0)
    hot = one_hot_rows(own_ids, first_slot, grad_window.shape[0])
    token_sums = jnp.einsum("htn,nhc->htc", hot, grad_window, preferred_element_type=jnp.float32)
    padded_len = jnp.concatenate([jnp.ones((id_heads, 1), jnp.int32), slot_len], axis=1)
    window_len = lax.dynamic_slice_in_dim(padded_len, first_slot + 1, slot_count + 1, 1).astype(
        jnp.float32
    )
    relative_ids = own_ids - first_slot
    window_cols = jnp.arange(slot_count + 1, dtype=jnp.int32)
    token_len = jnp.sum(
        jnp.where(
            relative_ids[:, :, None] == window_cols[None, None, :], window_len[:, None, :], 0.0
        ),
        axis=2,
    )[:, :, None]
    token_grads = token_sums / token_len
    key_back, value_back = (
        lax.all_to_all(
            token_grads[:, :, :head_dim].astype(jnp.bfloat16),
            "head",
            split_axis=1,
            concat_axis=0,
            tiled=True,
        ).astype(jnp.float32),
        lax.all_to_all(
            token_grads[:, :, head_dim:].astype(jnp.bfloat16),
            "head",
            split_axis=1,
            concat_axis=0,
            tiled=True,
        ).astype(jnp.float32),
    )
    return (out_back, key_back, value_back)


def solution(mesh):
    placed = (
        P(None, ("ctx", "head"), None),
        P(None, ("ctx", "head"), None),
        P(None, ("ctx", "head"), None, None),
        P(None, ("ctx", "head"), None, None),
        P("head", None),
    )
    return jax.shard_map(
        per_device,
        mesh=mesh,
        in_specs=placed,
        out_specs=(
            P(None, ("ctx", "head"), None, None),
            P(None, ("ctx", "head"), None),
            P(None, ("ctx", "head"), None),
        ),
        check_vma=False,
    )
```

profile of v0, /device:TPU:15, one launch (start us, length us, event | category | flops | bytes accessed | tf_op | source)
XLA Modules:
  0.0 238.5 jit_solution(12412605172236448797)
XLA Ops:
  7.2 4.1 %all-to-all-start = ((bf16[8,64,128]{2,1,0:T(8,128)(2,1)}), bf16[8,64,128]{2,1,0:T(8,128)(2,1)S(1)}, u32[]{:S(2)}, u32[]{:S(2)}) async-start(bf16[8,64,128]{2,1,0:T(8,128)(2,1)} %param.11), calls=%async_computation | async-start | bytes 262144 | tf_op jit(solution)/shard_map/all_to_all | solution.py:28
  14.0 5.2 %all-to-all-start.1 = ((bf16[8,64,128]{2,1,0:T(8,128)(2,1)}), bf16[8,64,128]{2,1,0:T(8,128)(2,1)S(1)}, u32[]{:S(2)}, u32[]{:S(2)}) async-start(bf16[8,64,128]{2,1,0:T(8,128)(2,1)} %param.12), calls=%async_computation.1 | async-start | bytes 262144 | tf_op jit(solution)/shard_map/all_to_all | solution.py:29
  19.2 2.7 %all-to-all-done.1 = bf16[8,64,128]{2,1,0:T(8,128)(2,1)S(1)} async-done(((bf16[8,64,128]{2,1,0:T(8,128)(2,1)}), bf16[8,64,128]{2,1,0:T(8,128)(2,1)S(1)}, u32[]{:S(2)}, u32[]{:S(2)}) %all-to-all-start.1) | async-done | bytes 131104 | tf_op jit(solution)/shard_map/all_to_all | solution.py:29
  21.9 5.4 %all-to-all-start.2 = ((bf16[8,64,8,128]{3,2,1,0:T(8,128)(2,1)}), bf16[8,64,8,128]{3,2,1,0:T(8,128)(2,1)S(1)}, u32[]{:S(2)}, u32[]{:S(2)}) async-start(bf16[8,64,8,128]{3,2,1,0:T(8,128)(2,1)} %param.13), calls=%async_computation.2 | async-start | bytes 2097152 | tf_op jit(solution)/shard_map/all_to_all | solution.py:30
  28.4 11.5 %all-to-all-done.2 = bf16[8,64,8,128]{3,2,1,0:T(8,128)(2,1)S(1)} async-done(((bf16[8,64,8,128]{3,2,1,0:T(8,128)(2,1)}), bf16[8,64,8,128]{3,2,1,0:T(8,128)(2,1)S(1)}, u32[]{:S(2)}, u32[]{:S(2)}) %all-to-all-start.2) | async-done | bytes 1048608 | tf_op jit(solution)/shard_map/all_to_all | solution.py:30
  39.9 6.1 %all-to-all-start.4 = ((bf16[8,64,8,128]{3,2,1,0:T(8,128)(2,1)}), bf16[8,64,8,128]{3,2,1,0:T(8,128)(2,1)}, u32[]{:S(2)}, u32[]{:S(2)}) async-start(bf16[8,64,8,128]{3,2,1,0:T(8,128)(2,1)} %param.14), calls=%async_computation.4 | async-start | bytes 2097152 | tf_op jit(solution)/shard_map/all_to_all | solution.py:31
  46.2 2.2 collective-permute-start
  49.1 2.3 collective-permute-done
  51.6 19.6 %all_gather.8 = bf16[512,2,128]{2,0,1:T(8,128)(2,1)S(1)} all-gather(bf16[64,2,128]{2,0,1:T(8,128)(2,1)S(1)} %slice.51), channel_id=1, replica_groups=mesh['ctx'=8,'head'=4] {'ctx'}, dimensions={0}, use_global_device_ids=true | all-gather | bytes 294912 | tf_op jit(solution)/shard_map/all_gather | solution.py:95
  71.2 25.5 %all_gather.7 = bf16[512,2,256]{2,0,1:T(8,128)(2,1)S(1)} all-gather(bf16[64,2,256]{2,0,1:T(8,128)(2,1)S(1)} %fusion.31), channel_id=1, replica_groups=mesh['ctx'=8,'head'=4] {'ctx'}, dimensions={0}, use_global_device_ids=true | all-gather | bytes 589824 | tf_op jit(solution)/shard_map/all_gather | solution.py:114
  96.9 4.9 %conditional.3 = (f32[2,2048]{1,0:T(2,128)}, f32[2,2048]{1,0:T(2,128)S(1)}) conditional(s32[]{:T(128)} %convert_element_type.72, () %tuple.34, (s32[2,8,64]{2,1,0:T(8,128)S(1)}, s32[256,8]{1,0:T(8,128)S(1)}, bf16[2,2048,128]{2,1,0:T(8,128)(2,1)S(1)}, bf16[512,2,128]{2,0,1:T(8,128)(2,1)S(1)}) %tuple.56), branch_computations={%region_2.3_spmd, %region_3.6_spmd} | conditional | flops 555741184 | bytes 18251792 | solution.py:104
  99.0 2.7 %fusion.1 = f32[2,2048]{1,0:T(2,128)S(1)} fusion(f32[2,2048,512]{1,2,0:T(8,128)S(1)} %get-tuple-element.122, f32[2,2048]{1,0:T(2,128)} %broadcast_maximum_fusion, s32[2048]{0:T(1024)S(1)} %le.37, s32[2,512]{1,0:T(2,128)S(1)} %le.35), kind=kLoop, calls=%fused_computation.3 | loop fusion | flops 10481664 | bytes 8433664 | tf_op jit(solution)/shard_map/cond/branch_1_fun/reduce_sum | solution.py:101
  103.2 3.5 %conditional.4 = (bf16[2,2048,128]{2,1,0:T(8,128)(2,1)S(1)}) conditional(s32[]{:T(128)} %convert_element_type.72, () %tuple.33, (s32[2,8,64]{2,1,0:T(8,128)S(1)}, s32[256,8]{1,0:T(8,128)S(1)}, bf16[512,2,256]{2,0,1:T(8,128)(2,1)S(1)}, bf16[2,2048,128]{2,1,0:T(8,128)(2,1)S(1)}, f32[2,2048]{1,0:T(2,128)}) %tuple.57), branch_computations={%region_6.7_spmd, %region_7.8_spmd} | conditional | flops 1084227584 | bytes 2674696 | solution.py:125
  103.4 3.3 %fusion.2 = bf16[2,2048,128]{2,1,0:T(8,128)(2,1)S(1)} fusion(bf16[2,2048,128]{2,1,0:T(8,128)(2,1)S(1)} %get-tuple-element.67, f32[2,2048]{1,0:T(2,128)} %get-tuple-element.69, s32[2,512]{1,0:T(2,128)S(1)} %le.50, s32[2048]{0:T(1024)S(1)} %le.52, bf16[512,2,256]{2,0,1:T(8,128)(2,1)S(1)} %get-tuple-element.68), kind=kOutput, calls=%fused_computation.6 | convolution fusion | flops 1084227584 | bytes 2650112 | tf_op jit(solution)/shard_map/cond/branch_1_fun/hrn,nhd->hrd/dot_general | solution.py:118
  106.9 21.8 %conditional.5 = (bf16[512,2,256]{0,2,1:T(8,128)(2,1)S(1)}) conditional(s32[]{:T(128)} %convert_element_type.72, () %tuple.37, (s32[2,8,64]{2,1,0:T(8,128)S(1)}, s32[256,8]{1,0:T(8,128)S(1)}, bf16[512,2,256]{2,0,1:T(8,128)(2,1)}, bf16[2,2048,128]{2,1,0:T(8,128)(2,1)}, f32[2,2048]{1,0:T(2,128)}, /*index=5*/bf16[2,4,64,8,128]{4,3,2,0,1:T(8,128)(2,1)}, ...), branch_computations={%region_8.9_spmd, %region_9.11_spmd} | conditional | flops 2175528960 | bytes 49414264 | solution.py:157
  110.1 5.9 %fusion.20 = f32[2,2048,512]{2,1,0:T(8,128)} fusion(bf16[2,2048,128]{2,1,0:T(8,128)(2,1)} %get-tuple-element.117, bf16[512,2,256]{2,0,1:T(8,128)(2,1)} %get-tuple-element.73), kind=kOutput, calls=%fused_computation.23 | convolution fusion | flops 536870912 | bytes 9699328 | tf_op jit(solution)/shard_map/cond/branch_1_fun/hrd,nhd->hrn/dot_general | solution.py:79
  116.0 7.0 %fusion.17 = bf16[512,2,128]{0,2,1:T(8,128)(2,1)S(1)} fusion(bf16[2,2048,128]{2,1,0:T(8,128)(2,1)S(1)} %copy-done.1, f32[2,2048,512]{2,1,0:T(8,128)} %fusion.20, bf16[2,2048,128]{2,1,0:T(8,128)(2,1)S(1)} %bitcast.57, f32[2,2048]{1,0:T(2,128)S(1)} %multiply_reduce_fusion, f32[2,2048]{1,0:T(2,128)} %get-tuple-element.74, s32[2,512]{1,0:T(2,128)S(1)} %copy-done.5, ...), kind=kOutput, calls=%fused_computation.20 | convolution fusion | flops 1088684032 | bytes 11055104 | tf_op jit(solution)/shard_map/cond/branch_1_fun/hrn,hrd->nhd/dot_general | solution.py:152
  123.0 5.6 %fusion.13 = bf16[512,2,128]{0,2,1:T(8,128)(2,1)S(1)} fusion(bf16[2,2048,128]{2,1,0:T(8,128)(2,1)S(1)} %bitcast.58, f32[2,2048,512]{2,1,0:T(8,128)} %fusion.20, f32[2,2048]{1,0:T(2,128)} %get-tuple-element.74, s32[2,512]{1,0:T(2,128)S(1)} %copy-done.5, s32[2048]{0:T(1024)S(1)} %le.57), kind=kOutput, calls=%fused_computation.18 | convolution fusion | flops 547356672 | bytes 9728000 | tf_op jit(solution)/shard_map/cond/branch_1_fun/hrn,hrd->nhd/dot_general | solution.py:141
  130.9 16.8 %all-to-all-start.3 = ((bf16[2,256,8,128]{3,2,0,1:T(8,128)(2,1)}), bf16[2,256,8,128]{3,2,0,1:T(8,128)(2,1)S(1)}, u32[]{:S(2)}, u32[]{:S(2)}) async-start(bf16[2,256,8,128]{3,2,0,1:T(8,128)(2,1)} %copy.58), calls=%async_computation.3 | async-start | bytes 2097152 | tf_op jit(solution)/shard_map/all_to_all | solution.py:127
  147.7 58.2 %reduce-scatter.2.cloned.1.call-done = bf16[64,2,256]{2,0,1:T(8,128)(2,1)} async-done(((bf16[512,2,256]{2,0,1:T(8,128)(2,1)}), bf16[64,2,256]{2,0,1:T(8,128)(2,1)}) %reduce-scatter.2.cloned.1.call-update) | async-done | bytes 65552 | tf_op jit(solution)/shard_map/reduce_scatter | solution.py:160
  206.6 2.3 collective-permute-start.1
  209.0 2.0 collective-permute-done.1
  212.9 7.2 %all-to-all-start.6 = ((bf16[2,256,128]{2,0,1:T(2,128)(2,1)}), bf16[2,256,128]{2,0,1:T(2,128)(2,1)S(1)}, u32[]{:S(2)}, u32[]{:S(2)}) async-start(bf16[2,256,128]{2,0,1:T(2,128)(2,1)} %copy.66), calls=%async_computation.7 | async-start | bytes 262144 | tf_op jit(solution)/shard_map/all_to_all | solution.py:188
  222.9 5.2 %all-to-all-start.5 = ((bf16[2,256,128]{2,0,1:T(2,128)(2,1)}), bf16[2,256,128]{2,0,1:T(2,128)(2,1)S(1)}, u32[]{:S(2)}, u32[]{:S(2)}) async-start(bf16[2,256,128]{2,0,1:T(2,128)(2,1)} %copy.64), calls=%async_computation.6 | async-start | bytes 262144 | tf_op jit(solution)/shard_map/all_to_all | solution.py:181
  (70 shorter events, 22.4 us)
Async XLA Ops:
  7.2 6.9 %all-to-all-start = ((bf16[8,64,128]{2,1,0:T(8,128)(2,1)}), bf16[8,64,128]{2,1,0:T(8,128)(2,1)S(1)}, u32[]{:S(2)}, u32[]{:S(2)}) async-start(bf16[8,64,128]{2,1,0:T(8,128)(2,1)} %param.11), calls=%async_computation | async-start | bytes 262144 | tf_op jit(solution)/shard_map/all_to_all | solution.py:28
  14.0 7.9 %all-to-all-start.1 = ((bf16[8,64,128]{2,1,0:T(8,128)(2,1)}), bf16[8,64,128]{2,1,0:T(8,128)(2,1)S(1)}, u32[]{:S(2)}, u32[]{:S(2)}) async-start(bf16[8,64,128]{2,1,0:T(8,128)(2,1)} %param.12), calls=%async_computation.1 | async-start | bytes 262144 | tf_op jit(solution)/shard_map/all_to_all | solution.py:29
  21.9 18.0 %all-to-all-start.2 = ((bf16[8,64,8,128]{3,2,1,0:T(8,128)(2,1)}), bf16[8,64,8,128]{3,2,1,0:T(8,128)(2,1)S(1)}, u32[]{:S(2)}, u32[]{:S(2)}) async-start(bf16[8,64,8,128]{3,2,1,0:T(8,128)(2,1)} %param.13), calls=%async_computation.2 | async-start | bytes 2097152 | tf_op jit(solution)/shard_map/all_to_all | solution.py:30
  39.9 66.9 %all-to-all-start.4 = ((bf16[8,64,8,128]{3,2,1,0:T(8,128)(2,1)}), bf16[8,64,8,128]{3,2,1,0:T(8,128)(2,1)}, u32[]{:S(2)}, u32[]{:S(2)}) async-start(bf16[8,64,8,128]{3,2,1,0:T(8,128)(2,1)} %param.14), calls=%async_computation.4 | async-start | bytes 2097152 | tf_op jit(solution)/shard_map/all_to_all | solution.py:31
  46.0 159.9 %reduce-scatter.2.cloned.1.call-start = ((), (), s32[]{:S(2)}) async-start(), calls=%async_computation.8 | async-start | bytes 589824 | tf_op jit(solution)/shard_map/reduce_scatter | solution.py:160
  46.2 5.2 %collective-permute-start = (f32[1,2,256]{2,0,1:T(1,128)S(1)}, f32[1,2,256]{2,0,1:T(1,128)S(1)}, u32[]{:S(2)}, u32[]{:S(2)}) collective-permute-start(f32[1,2,256]{2,0,1:T(1,128)S(1)} %slice.50), channel_id=1, source_target_pairs={{4,0},{8,4},{12,8},{16,12},{20,16},{24,20},{28,24},{5,1},{9,5},{13... | collective-permute-start | bytes 6152 | tf_op jit(solution)/shard_map/ppermute | solution.py:17
  96.7 6.5 %copy-start.4 = (bf16[512,2,256]{2,0,1:T(8,128)(2,1)}, bf16[512,2,256]{2,0,1:T(8,128)(2,1)S(1)}, u32[]{:S(2)}) copy-start(bf16[512,2,256]{2,0,1:T(8,128)(2,1)S(1)} %all_gather.7) | copy-start | bytes 1572868
  96.8 6.4 %copy-start = (bf16[2,4,64,8,128]{4,3,2,1,0:T(8,128)(2,1)}, bf16[2,4,64,8,128]{4,3,2,1,0:T(8,128)(2,1)S(1)}, u32[]{:S(2)}) copy-start(bf16[2,4,64,8,128]{4,3,2,1,0:T(8,128)(2,1)S(1)} %copy.57) | copy-start | bytes 3145732
  107.8 8.2 %copy-start.5 = (s32[2,512]{1,0:T(2,128)S(1)}, s32[2,512]{1,0:T(2,128)}, u32[]{:S(2)}) copy-start(s32[2,512]{1,0:T(2,128)} %le.55) | copy-start | bytes 12292 | tf_op jit(solution)/shard_map/cond
  109.2 1.0 copy-start.2
  110.1 5.9 %copy-start.1 = (bf16[2,2048,128]{2,1,0:T(8,128)(2,1)S(1)}, bf16[2,2048,128]{2,1,0:T(8,128)(2,1)}, u32[]{:S(2)}) copy-start(bf16[2,2048,128]{2,1,0:T(8,128)(2,1)} %get-tuple-element.117) | copy-start | bytes 3145732 | tf_op jit(solution)/shard_map/cond
  110.1 5.9 %copy-start.3 = (bf16[2,4,64,8,128]{4,3,2,1,0:T(8,128)(2,1)S(1)}, bf16[2,4,64,8,128]{4,3,2,1,0:T(8,128)(2,1)}, u32[]{:S(2)}) copy-start(bf16[2,4,64,8,128]{4,3,2,1,0:T(8,128)(2,1)} %copy-done.2) | copy-start | bytes 3145732 | tf_op jit(solution)/shard_map/cond
  130.9 82.1 %all-to-all-start.3 = ((bf16[2,256,8,128]{3,2,0,1:T(8,128)(2,1)}), bf16[2,256,8,128]{3,2,0,1:T(8,128)(2,1)S(1)}, u32[]{:S(2)}, u32[]{:S(2)}) async-start(bf16[2,256,8,128]{3,2,0,1:T(8,128)(2,1)} %copy.58), calls=%async_computation.3 | async-start | bytes 2097152 | tf_op jit(solution)/shard_map/all_to_all | solution.py:127
  206.6 4.3 %collective-permute-start.1 = (bf16[1,2,256]{2,0,1:T(2,128)(2,1)S(1)}, bf16[1,2,256]{2,0,1:T(2,128)(2,1)S(1)}, u32[]{:S(2)}, u32[]{:S(2)}) collective-permute-start(bf16[1,2,256]{2,0,1:T(2,128)(2,1)S(1)} %slice.52), channel_id=1, source_target_pairs={{0,4},{4,8},{8,12},{12,16},{16,20},{20,24},{24,28},{1,5},{5,9},{9,... | collective-permute-start | bytes 3080 | tf_op jit(solution)/shard_map/ppermute | solution.py:17
  212.9 10.0 %all-to-all-start.6 = ((bf16[2,256,128]{2,0,1:T(2,128)(2,1)}), bf16[2,256,128]{2,0,1:T(2,128)(2,1)S(1)}, u32[]{:S(2)}, u32[]{:S(2)}) async-start(bf16[2,256,128]{2,0,1:T(2,128)(2,1)} %copy.66), calls=%async_computation.7 | async-start | bytes 262144 | tf_op jit(solution)/shard_map/all_to_all | solution.py:188
  222.9 7.9 %all-to-all-start.5 = ((bf16[2,256,128]{2,0,1:T(2,128)(2,1)}), bf16[2,256,128]{2,0,1:T(2,128)(2,1)S(1)}, u32[]{:S(2)}, u32[]{:S(2)}) async-start(bf16[2,256,128]{2,0,1:T(2,128)(2,1)} %copy.64), calls=%async_computation.6 | async-start | bytes 262144 | tf_op jit(solution)/shard_map/all_to_all | solution.py:181
Sparse Core Ops, SparseCore 0:
  129.8 76.0 reduce-scatter.1
where the time goes:
time: 242 us; the launch traced here: 238 us
  waiting for transfers between devices  80.2 us (33%)
  starting transfers between devices  54.6 us (23%)
  blocking collectives  45.1 us (19%)
  matrix products  24.4 us (10%)
  between operations  14.8 us (6%)
  local copies, waits for them, and re-layouts  11 us (5%)
  other arithmetic  8.09 us (3%)
    reduce_scatter x1, waiting for transfers between devices, per_device(): lax.psum_scatter(partials.astype(jnp.bfloat16), 'ctx', scatter_dimension=...  58.2 us
    all_gather x1, blocking collectives, per_device(): pair_block = lax.all_gather(slot_pairs, 'ctx', axis=0, tiled=True)  25.5 us
    all_gather x1, blocking collectives, per_device(): lax.all_gather(slot_pairs[:, :, :head_dim], 'ctx', axis=0, tiled=True)  19.6 us
    all_to_all x1, starting transfers between devices, per_device(): lax.all_to_all(attended.reshape(local_heads, query_count, group_size, hea...  16.8 us
    all_to_all x1, waiting for transfers between devices, per_device(): lax.all_to_all(queries, 'head', split_axis=0, concat_axis=1, tiled=True)  11.5 us
    all_to_all x1, starting transfers between devices, per_device(): lax.all_to_all(token_grads[:, :, head_dim:].astype(jnp.bfloat16), 'head',...  7.25 us
    dot_general x2, matrix products, block_scores(): jnp.einsum('hrd,nhd->hrn', query_rows, key_block, preferred_element_type=...  7.22 us
    dot_general x1, matrix products, grad_advance(): jnp.einsum('hrn,hrd->nhd', dscores, query_rows, preferred_element_type=jn...  6.96 us
  transfers between devices with their start and end apart: 10, of which 8 were waited for; matrix products, arithmetic and copies ran while one was open for 8% of the time, Pallas kernels for 0%

commit v1 on v0

v1 whole, which is shorter than its diff:
```python
import functools
import math

import jax
import jax.numpy as jnp
from jax import lax
from jax.experimental import pallas as pl
from jax.experimental.pallas import tpu as pltpu
from jax.sharding import PartitionSpec as P

RATIO = 4
EDGE = 16
LANES = 128
MESH = pl.DeviceIdType.MESH
neg_big = -1e30


def dot_nt(a, b):
    return lax.dot_general(a, b, (((1,), (1,)), ((), ())), preferred_element_type=jnp.float32)


def dot_tn(a, b):
    return lax.dot_general(a, b, (((0,), (0,)), ((), ())), preferred_element_type=jnp.float32)


def dot_nn(a, b):
    return lax.dot_general(a, b, (((1,), (0,)), ((), ())), preferred_element_type=jnp.float32)


def kernel(
    dims,
    q_ref, g_ref, k_ref, v_ref, id_ref, thr_ref,
    out_ref, kg_ref, vg_ref,
    qb, gb, tk, tv, ek, ev, thrb, pairs, att, part, rs, acc, tg, tgx, rt, rx,
    q_s, q_r, g_s, g_r, loc, tok_s, tok_r, ext_s, ext_r, thr_s, thr_r,
    ag_s, ag_r, fw_s, fw_r, at_s, at_r, rs_s, rs_r, tg_s, tg_r, tx_s, tx_r,
):
    nc, nh, hpd, T, R, S, D = dims
    ny = nh // 2
    TB = T * nh
    NS = nc * S
    scale = 1.0 / math.sqrt(D)
    ctx = lax.axis_index("ctx")
    j = lax.axis_index("head")
    y, c = j // 2, lax.rem(j, 2)
    peer = y * 2 + 1 - c

    def remote(src, dst, ssem, rsem, to_ctx, to_head):
        return pltpu.make_async_remote_copy(
            src_ref=src, dst_ref=dst, send_sem=ssem, recv_sem=rsem,
            device_id=(to_ctx, to_head), device_id_type=MESH,
        )

    def heads(ref, owner):
        return ref.at[pl.ds(owner * hpd, hpd)]

    ek[...] = jnp.zeros_like(ek)
    ev[...] = jnp.zeros_like(ev)
    rx[...] = jnp.zeros_like(rx)

    @pl.loop(0, nc)
    def _(b):
        @pl.when(b > ctx)
        def _():
            for yy in range(ny):
                for h in range(hpd):
                    pairs[yy, h, b] = jnp.zeros((S, 2 * D), jnp.bfloat16)

    barrier = pltpu.get_barrier_semaphore()
    me = ctx * nh + j

    @pl.loop(1, nc * nh)
    def _(i):
        other = lax.rem(me + i, nc * nh)
        pl.semaphore_signal(
            barrier, inc=1, device_id=(other // nh, lax.rem(other, nh)), device_id_type=MESH
        )

    pl.semaphore_wait(barrier, nc * nh - 1)

    def tok_copy(to, frm, kv):
        src, dst = ((k_ref, tk), (v_ref, tv))[kv]
        return remote(heads(src, to), dst.at[:, frm], tok_s.at[to, kv], tok_r.at[frm, kv], ctx, to)

    def ext_copy(to_ctx, to, kv):
        src, dst = ((k_ref, ek), (v_ref, ev))[kv]
        return remote(
            src.at[pl.ds(to * hpd, hpd), pl.ds(0, EDGE)], dst.at[:, pl.ds(0, EDGE)],
            ext_s.at[to, kv], ext_r.at[kv], to_ctx, to,
        )

    def thr_copy(to_y, frm_y):
        return remote(thr_ref.at[to_y], thrb.at[frm_y], thr_s.at[to_y], thr_r.at[frm_y], ctx, to_y * 2 + c)

    def swap_copy(yy, kv, core):
        src, dst, ss, sr = ((q_ref, qb, q_s, q_r), (g_ref, gb, g_s, g_r))[kv]
        return remote(
            heads(src, yy * 2 + 1 - c), dst.at[yy, :, core], ss.at[yy], sr.at[yy], ctx, peer
        )

    def ag_copy(to_ctx, frm):
        blk = pairs.at[y, :, frm]
        return remote(blk, blk, ag_s.at[to_ctx], ag_r.at[frm], to_ctx, j)

    def fw_copy(to_y, frm_y, b):
        blk = pairs.at[frm_y, :, b]
        return remote(blk, blk, fw_s.at[to_y, b], fw_r.at[frm_y, b], ctx, to_y * 2 + c)

    def att_copy(yy):
        return remote(att.at[yy, :, 1 - c], heads(out_ref, yy * 2 + c), at_s.at[yy], at_r.at[yy], ctx, peer)

    def att_in(yy):
        return remote(att.at[yy, :, 1 - c], heads(out_ref, yy * 2 + 1 - c), at_s.at[yy], at_r.at[yy], ctx, peer)

    def rs_copy(yy, b, frm_ctx, frm_y):
        return remote(
            part.at[yy, :, b], rs.at[frm_ctx, frm_y], rs_s.at[yy, b], rs_r.at[frm_ctx, frm_y], b, yy * 2 + c
        )

    def tg_copy(to, frm):
        return remote(tg.at[to], rt.at[frm], tg_s.at[to], tg_r.at[frm], ctx, to)

    def tx_copy(to_ctx, frm):
        return remote(tgx, rx.at[frm], tx_s, tx_r.at[frm], to_ctx, 0)

    for d in range(1, nh):
        to = lax.rem(j + d, nh)
        tok_copy(to, j, 0).start()
        tok_copy(to, j, 1).start()

    @pl.when((j == 0) & (ctx > 0))
    def _():
        for to in range(nh):
            ext_copy(ctx - 1, to, 0).start()
            ext_copy(ctx - 1, to, 1).start()

    own_tok = [
        pltpu.make_async_copy(heads(k_ref, j), tk.at[:, j], loc.at[0]),
        pltpu.make_async_copy(heads(v_ref, j), tv.at[:, j], loc.at[1]),
    ]
    own_thr = pltpu.make_async_copy(thr_ref.at[y], thrb.at[y], loc.at[2])
    for cp in own_tok:
        cp.start()
    own_thr.start()
    for d in range(1, ny):
        thr_copy(lax.rem(y + d, ny), y).start()
    own_rows = []
    for d in range(ny):
        yy = lax.rem(y + d, ny)
        swap_copy(yy, 0, c).start()
        swap_copy(yy, 1, c).start()
        own_rows.append(
            pltpu.make_async_copy(heads(q_ref, yy * 2 + c), qb.at[yy, :, c], loc.at[3 + 2 * d])
        )
        own_rows.append(
            pltpu.make_async_copy(heads(g_ref, yy * 2 + c), gb.at[yy, :, c], loc.at[4 + 2 * d])
        )
    for cp in own_rows:
        cp.start()

    for d in range(1, nh):
        frm = lax.rem(j + d, nh)
        tok_copy(j, frm, 0).wait_recv()
        tok_copy(j, frm, 1).wait_recv()

    @pl.when(ctx < nc - 1)
    def _():
        ext_copy(ctx, j, 0).wait_recv()
        ext_copy(ctx, j, 1).wait_recv()

    for cp in own_tok:
        cp.wait()

    def hot(h):
        rel = id_ref[h]
        main = lax.broadcasted_iota(jnp.int32, (S, TB), 0) == rel[:, :TB]
        edge = lax.broadcasted_iota(jnp.int32, (S, LANES), 0) == rel[:, TB:]
        main, edge = main.astype(jnp.float32), edge.astype(jnp.float32)
        count = jnp.sum(main, axis=1, keepdims=True) + jnp.sum(edge, axis=1, keepdims=True)
        return main.astype(jnp.bfloat16), edge.astype(jnp.bfloat16), count

    for h in range(hpd):
        main, edge, count = hot(h)
        keys = dot_nn(main, tk[h].reshape(TB, D)) + dot_nn(edge, ek[h])
        vals = dot_nn(main, tv[h].reshape(TB, D)) + dot_nn(edge, ev[h])
        pairs[y, h, ctx, :, :D] = (keys / count).astype(jnp.bfloat16)
        pairs[y, h, ctx, :, D:] = (vals / count).astype(jnp.bfloat16)

    @pl.loop(0, nc)
    def _(i):
        to = nc - 1 - i

        @pl.when(to > ctx)
        def _():
            ag_copy(to, ctx).start()

    for d in range(1, ny):
        fw_copy(lax.rem(y + d, ny), y, ctx).start()

    for cp in own_rows:
        cp.wait()
    own_thr.wait()
    for d in range(ny):
        yy = lax.rem(y + d, ny)
        swap_copy(yy, 0, 1 - c).wait_recv()
        swap_copy(yy, 1, 1 - c).wait_recv()

    @pl.loop(0, nc)
    def _(i):
        b = nc - 1 - i

        @pl.when(b < ctx)
        def _():
            ag_copy(ctx, b).wait_recv()
            for d in range(1, ny):
                fw_copy(lax.rem(y + d, ny), y, b).start()

    @pl.loop(0, ny)
    def _(k):
        yy = lax.rem(y + k, ny)

        @pl.when(k > 0)
        def _():
            thr_copy(y, yy).wait_recv()

            @pl.loop(0, nc)
            def _(b):
                @pl.when(b <= ctx)
                def _():
                    fw_copy(y, yy, b).wait_recv()

        @pl.loop(0, hpd)
        def _(h):
            both = pairs[yy, h].reshape(NS, 2 * D)
            keys, vals = both[:, :D], both[:, D:]
            slot = lax.broadcasted_iota(jnp.int32, (NS, R), 0)
            key_sum = val_sum = None
            for core in range(2):
                rows, grads = qb[yy, h, core], gb[yy, h, core]
                scores = jnp.where(slot <= thrb[yy, h, core], dot_nt(keys, rows), neg_big)
                top = jnp.max(scores, axis=0, keepdims=True)
                raw = jnp.exp2((scores - top) * (scale * math.log2(math.e)))
                weights = raw * (1.0 / jnp.sum(raw, axis=0, keepdims=True))
                low = weights.astype(jnp.bfloat16)
                seen = dot_tn(vals, low).astype(jnp.bfloat16).astype(jnp.float32)
                grads_t = grads.astype(jnp.float32).T
                row_dot = jnp.sum(grads_t * seen, axis=0, keepdims=True)
                att[yy, h, core] = seen.T.astype(jnp.bfloat16)
                slope = (weights * (dot_nt(vals, grads) - row_dot)).astype(jnp.bfloat16)
                val_grad = dot_nn(low, grads)
                key_grad = dot_nn(slope, rows)
                key_sum = key_grad if key_sum is None else key_sum + key_grad
                val_sum = val_grad if val_sum is None else val_sum + val_grad
            part[yy, h, :, :, :D] = (key_sum * scale).astype(jnp.bfloat16).reshape(nc, S, D)
            part[yy, h, :, :, D:] = val_sum.astype(jnp.bfloat16).reshape(nc, S, D)

        @pl.loop(0, nc)
        def _(b):
            @pl.when((b < ctx) | ((b == ctx) & (k > 0)))
            def _():
                rs_copy(yy, b, ctx, y).start()

        att_copy(yy).start()
        pltpu.make_async_copy(att.at[yy, :, c], heads(out_ref, yy * 2 + c), loc.at[3 + yy]).start()

    for h in range(hpd):
        acc[h] = part[y, h, ctx].astype(jnp.float32)

    @pl.loop(0, nc)
    def _(b):
        for yy in range(ny):
            @pl.when((b > ctx) | ((b == ctx) & (y != yy)))
            def _():
                rs_copy(y, ctx, b, yy).wait_recv()
                for h in range(hpd):
                    acc[h] += rs[b, yy, h].astype(jnp.float32)

    for h in range(hpd):
        main, edge, count = hot(h)
        unit = (acc[h].astype(jnp.bfloat16).astype(jnp.float32) / count).astype(jnp.bfloat16)
        spread = dot_tn(main, unit).astype(jnp.bfloat16)
        for to in range(nh):
            tg[to, h] = spread[to * T:(to + 1) * T]
        tgx[h] = dot_tn(edge, unit)[:EDGE].astype(jnp.bfloat16)

    for d in range(1, nh):
        tg_copy(lax.rem(j + d, nh), j).start()

    @pl.when((ctx < nc - 1))
    def _():
        @pl.when((ctx >= 0))
        def _():
            tx_copy(ctx + 1, j).start()

    own_tg = pltpu.make_async_copy(tg.at[j], rt.at[j], loc.at[0])
    own_tg.start()

    for d in range(1, nh):
        to = lax.rem(j + d, nh)
        tok_copy(to, j, 0).wait_send()
        tok_copy(to, j, 1).wait_send()

    @pl.when((j == 0) & (ctx > 0))
    def _():
        for to in range(nh):
            ext_copy(ctx - 1, to, 0).wait_send()
            ext_copy(ctx - 1, to, 1).wait_send()

    for d in range(1, ny):
        thr_copy(lax.rem(y + d, ny), y).wait_send()
    for yy in range(ny):
        swap_copy(yy, 0, c).wait_send()
        swap_copy(yy, 1, c).wait_send()
        att_copy(yy).wait_send()
        att_in(yy).wait_recv()
        pltpu.make_async_copy(att.at[yy, :, c], heads(out_ref, yy * 2 + c), loc.at[3 + yy]).wait()

    @pl.loop(0, nc)
    def _(b):
        @pl.when(b > ctx)
        def _():
            ag_copy(b, ctx).wait_send()

        @pl.when(b <= ctx)
        def _():
            for d in range(1, ny):
                yy = lax.rem(y + d, ny)
                fw_copy(yy, y, b).wait_send()
                rs_copy(yy, b, ctx, y).wait_send()

        @pl.when(b < ctx)
        def _():
            rs_copy(y, b, ctx, y).wait_send()

    own_tg.wait()
    for d in range(1, nh):
        tg_copy(j, lax.rem(j + d, nh)).wait_recv()
    for owner in range(nh):
        for h in range(hpd):
            rows = rt[owner, h].astype(jnp.float32)
            kg_ref[owner * hpd + h] = rows[:, :D]
            vg_ref[owner * hpd + h] = rows[:, D:]

    @pl.when((j == 0) & (ctx > 0))
    def _():
        for owner in range(nh):
            tx_copy(ctx, owner).wait_recv()
            for h in range(hpd):
                rows = rx[owner, h].astype(jnp.float32)
                kg_ref[owner * hpd + h, :EDGE] += rows[:, :D]
                vg_ref[owner * hpd + h, :EDGE] += rows[:, D:]

    for d in range(1, nh):
        tg_copy(lax.rem(j + d, nh), j).wait_send()

    @pl.when((ctx < nc - 1))
    def _():
        tx_copy(ctx + 1, j).wait_send()


def per_device(nc, nh, token_keys, token_values, queries, out_grad, slot_ids):
    heads_all, T, D = token_keys.shape
    group = queries.shape[2]
    hpd, context = slot_ids.shape
    R = queries.shape[1] * group
    stride = T // queries.shape[1]
    TB = T * nh
    S = TB // RATIO
    ny = nh // 2
    ctx = lax.axis_index("ctx")
    padded = jnp.pad(slot_ids, ((0, 0), (0, LANES)), constant_values=context)
    window = lax.dynamic_slice_in_dim(padded, ctx * TB, TB + LANES, 1)
    relative = (window - ctx * S).reshape(hpd, 1, TB + LANES)
    seen_at = window[:, stride - 1:TB:stride]
    limit = jnp.repeat(seen_at.reshape(hpd, ny, 2, 1, R // group), group, axis=4)
    limit = limit.transpose(1, 0, 2, 3, 4)
    bf, f32 = jnp.bfloat16, jnp.float32
    dma = pltpu.SemaphoreType.DMA
    anywhere = pl.BlockSpec(memory_space=pl.ANY)
    vmem = pl.BlockSpec(memory_space=pltpu.VMEM)
    attended, key_grad, value_grad = pl.pallas_call(
        functools.partial(kernel, (nc, nh, hpd, T, R, S, D)),
        out_shape=(
            jax.ShapeDtypeStruct((heads_all, R, D), bf),
            jax.ShapeDtypeStruct((heads_all, T, D), f32),
            jax.ShapeDtypeStruct((heads_all, T, D), f32),
        ),
        in_specs=[anywhere] * 4 + [vmem, vmem],
        out_specs=(anywhere, vmem, vmem),
        scratch_shapes=[
            pltpu.VMEM((ny, hpd, 2, R, D), bf),
            pltpu.VMEM((ny, hpd, 2, R, D), bf),
            pltpu.VMEM((hpd, nh, T, D), bf),
            pltpu.VMEM((hpd, nh, T, D), bf),
            pltpu.VMEM((hpd, LANES, D), bf),
            pltpu.VMEM((hpd, LANES, D), bf),
            pltpu.VMEM((ny, hpd, 2, 1, R), jnp.int32),
            pltpu.VMEM((ny, hpd, nc, S, 2 * D), bf),
            pltpu.VMEM((ny, hpd, 2, R, D), bf),
            pltpu.VMEM((ny, hpd, nc, S, 2 * D), bf),
            pltpu.VMEM((nc, ny, hpd, S, 2 * D), bf),
            pltpu.VMEM((hpd, S, 2 * D), f32),
            pltpu.VMEM((nh, hpd, T, 2 * D), bf),
            pltpu.VMEM((hpd, EDGE, 2 * D), bf),
            pltpu.VMEM((nh, hpd, T, 2 * D), bf),
            pltpu.VMEM((nh, hpd, EDGE, 2 * D), bf),
            dma((ny,)), dma((ny,)), dma((ny,)), dma((ny,)), dma((3 + 2 * ny,)),
            dma((nh, 2)), dma((nh, 2)), dma((nh, 2)), dma((2,)), dma((ny,)), dma((ny,)),
            dma((nc,)), dma((nc,)), dma((ny, nc)), dma((ny, nc)), dma((ny,)), dma((ny,)),
            dma((ny, nc)), dma((nc, ny)), dma((nh,)), dma((nh,)), dma(()), dma((nh,)),
        ],
        compiler_params=pltpu.CompilerParams(
            collective_id=0, has_side_effects=True, vmem_limit_bytes=56 << 20
        ),
    )(
        queries.reshape(heads_all, R, D), out_grad.reshape(heads_all, R, D),
        token_keys, token_values, relative, limit,
    )
    return attended.reshape(queries.shape), key_grad, value_grad


def solution(mesh):
    nc, nh = mesh.shape["ctx"], mesh.shape["head"]
    rows = P(None, ("ctx", "head"), None)
    grouped = P(None, ("ctx", "head"), None, None)
    return jax.shard_map(
        functools.partial(per_device, nc, nh),
        mesh=mesh,
        in_specs=(rows, rows, grouped, grouped, P("head", None)),
        out_specs=(grouped, rows, rows),
        check_vma=False,
    )
```

time: 242 us -> 66.3 us (0.27); the launches traced: 238 us -> 65.9 us
  waiting for transfers between devices: 80.2 us -> 0 us
  Pallas kernels: 0 us -> 58.9 us
  starting transfers between devices: 54.6 us -> 0 us
  blocking collectives: 45.1 us -> 0 us
  matrix products: 24.4 us -> 0 us
  between operations: 14.8 us -> 0.68 us
  other arithmetic: 8.09 us -> 0.01 us
  local copies, waits for them, and re-layouts: 11 us -> 6.35 us
    pallas_call x0 -> x1, Pallas kernels: none -> 58.9 us  [per_device(): pl.pallas_call(functools.partial(kernel, (nc, nh, hpd, T, R, S, D)), out_...]
    reduce_scatter x1 -> x0, waiting for transfers between devices: 58.2 us -> none  [per_device(): lax.psum_scatter(partials.astype(jnp.bfloat16), 'ctx', scatter_dimension=...]
    all_to_all x7 -> x0, starting transfers between devices: 50.1 us -> none  [the longest x1 16.8 us: per_device(): lax.all_to_all(attended.reshape(local_heads, query_count, group_size, hea...]
    all_gather x2 -> x0, blocking collectives: 45.1 us -> none  [the longest x1 25.5 us: per_device(): pair_block = lax.all_gather(slot_pairs, 'ctx', axis=0, tiled=True)]
    dot_general x7 -> x0, matrix products: 24.4 us -> none  [the longest x2 7.22 us: block_scores(): jnp.einsum('hrd,nhd->hrn', query_rows, key_block, preferred_element_type=...]
    all_to_all x7 -> x0, waiting for transfers between devices: 17.7 us -> none  [the longest x1 11.5 us: per_device(): lax.all_to_all(queries, 'head', split_axis=0, concat_axis=1, tiled=True)]
    ppermute x2 -> x0, starting transfers between devices: 4.42 us -> none  [from_behind(): lax.ppermute(value, axis, [(source, source + steps) for source in range(i...]
    ppermute x2 -> x0, waiting for transfers between devices: 4.28 us -> none  [from_behind(): lax.ppermute(value, axis, [(source, source + steps) for source in range(i...]
  transfers between devices with their start and end apart: 10 -> 0, of which waited for: 8 -> 0; matrix products, arithmetic and copies ran while one was open for 8% -> 0% of each run, Pallas kernels for 0% -> 0%
where the time goes in v1:
time: 66.3 us; the launch traced here: 65.9 us
  Pallas kernels  58.9 us (89%)
  local copies, waits for them, and re-layouts  6.35 us (10%)
  between operations  0.68 us (1%)
    pallas_call x1, Pallas kernels, per_device(): pl.pallas_call(functools.partial(kernel, (nc, nh, hpd, T, R, S, D)), out_...  58.9 us
    unnamed x9, local copies, waits for them, and re-layouts  4.77 us

profile of v1, /device:TPU:15, one launch (start us, length us, event | category | flops | bytes accessed | tf_op | source)
XLA Modules:
  0.0 65.9 jit_solution(9624340383345543224)
XLA Ops:
  0.6 0.0 copy-start.2
  0.6 0.7 %copy-done.2 = s32[2,2048]{1,0:T(2,128)S(1)} copy-done((s32[2,2048]{1,0:T(2,128)S(1)}, s32[2,2048]{1,0:T(2,128)}, u32[]{:S(2)}) %copy-start.2) | copy-done | bytes 16408
  1.4 0.6 reshape.29.id_ref
  2.0 0.1 reshape.30
  2.0 0.1 broadcast_in_dim.5
  2.2 0.2 broadcast_in_dim.6
  2.3 0.6 copy.11
  3.0 58.9 %shard_map.76 = (bf16[8,512,128]{2,1,0:T(8,128)(2,1)}, f32[8,64,128]{2,1,0:T(8,128)}, f32[8,64,128]{2,1,0:T(8,128)}) custom-call(bf16[8,512,128]{2,1,0:T(8,128)(2,1)} %bitcast.8, bf16[8,512,128]{2,1,0:T(8,128)(2,1)} %bitcast.9, bf16[8,64,128]{2,1,0:T(8,128)(2,1)} %k_ref.1, bf16[8,64,128]{2,1,0:T(8,128)(2,1)} %v_ref.1, s32[2,1,384]{2,1,0:T(1,128)} %reshape.29.id_ref, ...), custom_call_target="tpu_custom_call" | custom-call | tf_op jit(solution)/shard_map/pallas_call | solution.py:381
  61.8 0.0 copy-start.1
  61.9 2.3 %copy.15 = bf16[8,64,8,128]{3,2,1,0:T(8,128)(2,1)} copy(bf16[8,64,8,128]{3,2,1,0:T(8,128)(2,1)} %bitcast.10) | data formatting | bytes 2097152
  64.2 0.0 copy-done.1
  64.2 0.0 copy-start
  64.2 0.7 %copy.16 = f32[8,64,128]{2,1,0:T(8,128)} copy(f32[8,64,128]{2,1,0:T(8,128)S(1)} %copy-done.1) | data formatting | bytes 524288
  64.9 0.3 copy-done
  65.2 0.7 %copy.17 = f32[8,64,128]{2,1,0:T(8,128)} copy(f32[8,64,128]{2,1,0:T(8,128)S(1)} %copy-done) | data formatting | bytes 524288
  (2 shorter events, 0.0 us)
Async XLA Ops:
  0.6 0.7 %copy-start.2 = (s32[2,2048]{1,0:T(2,128)S(1)}, s32[2,2048]{1,0:T(2,128)}, u32[]{:S(2)}) copy-start(s32[2,2048]{1,0:T(2,128)} %param.9) | copy-start | bytes 49156
  61.8 2.3 %copy-start.1 = (f32[8,64,128]{2,1,0:T(8,128)S(1)}, f32[8,64,128]{2,1,0:T(8,128)}, u32[]{:S(2)}) copy-start(f32[8,64,128]{2,1,0:T(8,128)} %get-tuple-element.13) | copy-start | bytes 786436
  64.2 1.0 %copy-start = (f32[8,64,128]{2,1,0:T(8,128)S(1)}, f32[8,64,128]{2,1,0:T(8,128)}, u32[]{:S(2)}) copy-start(f32[8,64,128]{2,1,0:T(8,128)} %get-tuple-element.14) | copy-start | bytes 786436

commit v2 on v1

--- a/solution.py
+++ b/solution.py
@@ -31,12 +31,13 @@
     dims,
     q_ref, g_ref, k_ref, v_ref, id_ref, thr_ref,
     out_ref, kg_ref, vg_ref,
-    qb, gb, tk, tv, ek, ev, thrb, pairs, att, part, rs, acc, tg, tgx, rt, rx,
+    qb, gb, tk, tv, ek, ev, thrb, pk, pv, att, part, ys, rs, acc, tg, tgx, rt, rx,
     q_s, q_r, g_s, g_r, loc, tok_s, tok_r, ext_s, ext_r, thr_s, thr_r,
-    ag_s, ag_r, fw_s, fw_r, at_s, at_r, rs_s, rs_r, tg_s, tg_r, tx_s, tx_r,
+    ag_s, ag_r, kx_s, kx_r, ky_s, ky_r, vy_s, vy_r, vx_s, vx_r, at_s, at_r,
+    ys_s, ys_r, rs_s, rs_r, tg_s, tg_r, tx_s, tx_r,
 ):
-    nc, nh, hpd, T, R, S, D = dims
-    ny = nh // 2
+    nc, nx, nh, hpd, T, R, S, D = dims
+    ny, nz = nh // 2, nc // nx
     TB = T * nh
     NS = nc * S
     scale = 1.0 / math.sqrt(D)
@@ -44,6 +45,7 @@
     j = lax.axis_index("head")
     y, c = j // 2, lax.rem(j, 2)
     peer = y * 2 + 1 - c
+    z, x = ctx // nx, lax.rem(ctx, nx)
 
     def remote(src, dst, ssem, rsem, to_ctx, to_head):
         return pltpu.make_async_remote_copy(
@@ -64,7 +66,8 @@
         def _():
             for yy in range(ny):
                 for h in range(hpd):
-                    pairs[yy, h, b] = jnp.zeros((S, 2 * D), jnp.bfloat16)
+                    pk[yy, h, b] = jnp.zeros((S, D), jnp.bfloat16)
+                    pv[yy, h, b] = jnp.zeros((S, D), jnp.bfloat16)
 
     barrier = pltpu.get_barrier_semaphore()
     me = ctx * nh + j
@@ -98,13 +101,31 @@
             heads(src, yy * 2 + 1 - c), dst.at[yy, :, core], ss.at[yy], sr.at[yy], ctx, peer
         )
 
-    def ag_copy(to_ctx, frm):
-        blk = pairs.at[y, :, frm]
-        return remote(blk, blk, ag_s.at[to_ctx], ag_r.at[frm], to_ctx, j)
-
-    def fw_copy(to_y, frm_y, b):
-        blk = pairs.at[frm_y, :, b]
-        return remote(blk, blk, fw_s.at[to_y, b], fw_r.at[frm_y, b], ctx, to_y * 2 + c)
+    def ag_copy(to_z, frm_z, kv):
+        blk = (pk, pv)[kv].at[y, :, frm_z * nx + x]
+        return remote(blk, blk, ag_s.at[to_z, kv], ag_r.at[frm_z, kv], to_z * nx + x, j)
+
+    def kx_copy(to_x, frm_x, zs):
+        blk = pk.at[y, :, zs * nx + frm_x]
+        return remote(blk, blk, kx_s.at[to_x, zs], kx_r.at[frm_x, zs], z * nx + to_x, j)
+
+    def ky_copy(to_y, frm_y, b):
+        blk = pk.at[frm_y, :, b]
+        return remote(blk, blk, ky_s.at[to_y, b], ky_r.at[frm_y, b], ctx, to_y * 2 + c)
+
+    def vy_copy(to_y, frm_y, zs):
+        blk = pv.at[frm_y, :, zs * nx + x]
+        return remote(blk, blk, vy_s.at[to_y, zs], vy_r.at[frm_y, zs], ctx, to_y * 2 + c)
+
+    def vx_copy(to_x, frm_x, yy, zs):
+        blk = pv.at[yy, :, zs * nx + frm_x]
+        return remote(blk, blk, vx_s.at[to_x, yy, zs], vx_r.at[frm_x, yy, zs], z * nx + to_x, j)
+
+    def x_sees(to_x, zs):
+        return (zs < z) | ((zs == z) & (to_x > x))
+
+    def x_gives(frm_x, zs):
+        return (zs < z) | ((zs == z) & (frm_x < x))
 
     def att_copy(yy):
         return remote(att.at[yy, :, 1 - c], heads(out_ref, yy * 2 + c), at_s.at[yy], at_r.at[yy], ctx, peer)
@@ -112,10 +133,13 @@
     def att_in(yy):
         return remote(att.at[yy, :, 1 - c], heads(out_ref, yy * 2 + 1 - c), at_s.at[yy], at_r.at[yy], ctx, peer)
 
-    def rs_copy(yy, b, frm_ctx, frm_y):
+    def ys_copy(to_y, frm_y, h, b):
         return remote(
-            part.at[yy, :, b], rs.at[frm_ctx, frm_y], rs_s.at[yy, b], rs_r.at[frm_ctx, frm_y], b, yy * 2 + c
-        )
+            part.at[to_y, h, b], ys.at[frm_y, h, b], ys_s.at[to_y, h, b], ys_r.at[frm_y, h, b], ctx, to_y * 2 + c
+        )
+
+    def rs_copy(b, frm_ctx):
+        return remote(part.at[y, :, b], rs.at[frm_ctx], rs_s.at[b], rs_r.at[frm_ctx], b, j)
 
     def tg_copy(to, frm):
         return remote(tg.at[to], rt.at[frm], tg_s.at[to], tg_r.at[frm], ctx, to)
@@ -183,19 +207,39 @@
         main, edge, count = hot(h)
         keys = dot_nn(main, tk[h].reshape(TB, D)) + dot_nn(edge, ek[h])
         vals = dot_nn(main, tv[h].reshape(TB, D)) + dot_nn(edge, ev[h])
-        pairs[y, h, ctx, :, :D] = (keys / count).astype(jnp.bfloat16)
-        pairs[y, h, ctx, :, D:] = (vals / count).astype(jnp.bfloat16)
-
-    @pl.loop(0, nc)
+        pk[y, h, ctx] = (keys / count).astype(jnp.bfloat16)
+        pv[y, h, ctx] = (vals / count).astype(jnp.bfloat16)
+
+    def spread_block(zs):
+        for d in range(1, nx):
+            to = lax.rem(x + d, nx)
+
+            @pl.when(x_sees(to, zs))
+            def _():
+                kx_copy(to, x, zs).start()
+
+        for d in range(1, ny):
+            to = lax.rem(y + d, ny)
+            vy_copy(to, y, zs).start()
+            ky_copy(to, y, zs * nx + x).start()
+
+        for d in range(1, nx):
+            to = lax.rem(x + d, nx)
+
+            @pl.when(x_sees(to, zs))
+            def _():
+                vx_copy(to, x, y, zs).start()
+
+    @pl.loop(0, nz)
     def _(i):
-        to = nc - 1 - i
-
-        @pl.when(to > ctx)
-        def _():
-            ag_copy(to, ctx).start()
-
-    for d in range(1, ny):
-        fw_copy(lax.rem(y + d, ny), y, ctx).start()
+        to = nz - 1 - i
+
+        @pl.when(to > z)
+        def _():
+            ag_copy(to, z, 0).start()
+            ag_copy(to, z, 1).start()
+
+    spread_block(z)
 
     for cp in own_rows:
         cp.wait()
@@ -205,15 +249,50 @@
         swap_copy(yy, 0, 1 - c).wait_recv()
         swap_copy(yy, 1, 1 - c).wait_recv()
 
-    @pl.loop(0, nc)
+    @pl.loop(0, nz)
     def _(i):
-        b = nc - 1 - i
-
-        @pl.when(b < ctx)
-        def _():
-            ag_copy(ctx, b).wait_recv()
-            for d in range(1, ny):
-                fw_copy(lax.rem(y + d, ny), y, b).start()
+        zs = nz - 1 - i
+
+        @pl.when(zs < z)
+        def _():
+            ag_copy(z, zs, 0).wait_recv()
+            ag_copy(z, zs, 1).wait_recv()
+            spread_block(zs)
+
+    @pl.loop(0, nz)
+    def _(i):
+        zs = nz - 1 - i
+
+        @pl.when(zs <= z)
+        def _():
+            for d in range(1, nx):
+                frm = lax.rem(x + d, nx)
+
+                @pl.when(x_gives(frm, zs))
+                def _():
+                    kx_copy(x, frm, zs).wait_recv()
+                    for e in range(1, ny):
+                        ky_copy(lax.rem(y + e, ny), y, zs * nx + frm).start()
+
+            for e in range(1, ny):
+                frm_y = lax.rem(y + e, ny)
+                vy_copy(y, frm_y, zs).wait_recv()
+                for d in range(1, nx):
+                    to = lax.rem(x + d, nx)
+
+                    @pl.when(x_sees(to, zs))
+                    def _():
+                        vx_copy(to, x, frm_y, zs).start()
+
+    def wait_vals(yy):
+        @pl.loop(0, nz)
+        def _(zs):
+            for d in range(1, nx):
+                frm = lax.rem(x + d, nx)
+
+                @pl.when(x_gives(frm, zs))
+                def _():
+                    vx_copy(x, frm, yy, zs).wait_recv()
 
     @pl.loop(0, ny)
     def _(k):
@@ -227,12 +306,13 @@
             def _(b):
                 @pl.when(b <= ctx)
                 def _():
-                    fw_copy(y, yy, b).wait_recv()
+                    ky_copy(y, yy, b).wait_recv()
+
+        wait_vals(yy)
 
         @pl.loop(0, hpd)
         def _(h):
-            both = pairs[yy, h].reshape(NS, 2 * D)
-            keys, vals = both[:, :D], both[:, D:]
+            keys, vals = pk[yy, h].reshape(NS, D), pv[yy, h].reshape(NS, D)
             slot = lax.broadcasted_iota(jnp.int32, (NS, R), 0)
             key_sum = val_sum = None
             for core in range(2):
@@ -254,26 +334,47 @@
             part[yy, h, :, :, :D] = (key_sum * scale).astype(jnp.bfloat16).reshape(nc, S, D)
             part[yy, h, :, :, D:] = val_sum.astype(jnp.bfloat16).reshape(nc, S, D)
 
-        @pl.loop(0, nc)
-        def _(b):
-            @pl.when((b < ctx) | ((b == ctx) & (k > 0)))
+            @pl.when(k > 0)
             def _():
-                rs_copy(yy, b, ctx, y).start()
+                @pl.loop(0, nc)
+                def _(b):
+                    @pl.when(b <= ctx)
+                    def _():
+                        ys_copy(yy, y, h, b).start()
 
         att_copy(yy).start()
         pltpu.make_async_copy(att.at[yy, :, c], heads(out_ref, yy * 2 + c), loc.at[3 + yy]).start()
 
-    for h in range(hpd):
-        acc[h] = part[y, h, ctx].astype(jnp.float32)
-
     @pl.loop(0, nc)
     def _(b):
-        for yy in range(ny):
-            @pl.when((b > ctx) | ((b == ctx) & (y != yy)))
-            def _():
-                rs_copy(y, ctx, b, yy).wait_recv()
-                for h in range(hpd):
-                    acc[h] += rs[b, yy, h].astype(jnp.float32)
+        @pl.when(b <= ctx)
+        def _():
+            for h in range(hpd):
+                total = part[y, h, b].astype(jnp.float32)
+                for d in range(1, ny):
+                    frm_y = lax.rem(y + d, ny)
+                    ys_copy(y, frm_y, h, b).wait_recv()
+                    total += ys[frm_y, h, b].astype(jnp.float32)
+
+                @pl.when(b < ctx)
+                def _():
+                    part[y, h, b] = total.astype(jnp.bfloat16)
+
+                @pl.when(b == ctx)
+                def _():
+                    acc[h] = total
+
+        @pl.when(b < ctx)
+        def _():
+            rs_copy(b, ctx).start()
+
+    @pl.loop(0, nc)
+    def _(b):
+        @pl.when(b > ctx)
+        def _():
+            rs_copy(ctx, b).wait_recv()
+            for h in range(hpd):
+                acc[h] += rs[b, h].astype(jnp.float32)
 
     for h in range(hpd):
         main, edge, count = hot(h)
@@ -315,22 +416,39 @@
         att_in(yy).wait_recv()
         pltpu.make_async_copy(att.at[yy, :, c], heads(out_ref, yy * 2 + c), loc.at[3 + yy]).wait()
 
+    @pl.loop(0, nz)
+    def _(zs):
+        @pl.when(zs > z)
+        def _():
+            ag_copy(zs, z, 0).wait_send()
+            ag_copy(zs, z, 1).wait_send()
+
+        @pl.when(zs <= z)
+        def _():
+            for d in range(1, ny):
+                vy_copy(lax.rem(y + d, ny), y, zs).wait_send()
+            for d in range(1, nx):
+                to = lax.rem(x + d, nx)
+
+                @pl.when(x_sees(to, zs))
+                def _():
+                    kx_copy(to, x, zs).wait_send()
+                    for yy in range(ny):
+                        vx_copy(to, x, yy, zs).wait_send()
+
     @pl.loop(0, nc)
     def _(b):
-        @pl.when(b > ctx)
-        def _():
-            ag_copy(b, ctx).wait_send()
-
         @pl.when(b <= ctx)
         def _():
             for d in range(1, ny):
                 yy = lax.rem(y + d, ny)
-                fw_copy(yy, y, b).wait_send()
-                rs_copy(yy, b, ctx, y).wait_send()
+                ky_copy(yy, y, b).wait_send()
+                for h in range(hpd):
+                    ys_copy(yy, y, h, b).wait_send()
 
         @pl.when(b < ctx)
         def _():
-            rs_copy(y, b, ctx, y).wait_send()
+            rs_copy(b, ctx).wait_send()
 
     own_tg.wait()
     for d in range(1, nh):
@@ -367,6 +485,8 @@
     TB = T * nh
     S = TB // RATIO
     ny = nh // 2
+    nx = 2 ** ((nc.bit_length() - 1) // 2)
+    nz = nc // nx
     ctx = lax.axis_index("ctx")
     padded = jnp.pad(slot_ids, ((0, 0), (0, LANES)), constant_values=context)
     window = lax.dynamic_slice_in_dim(padded, ctx * TB, TB + LANES, 1)
@@ -379,7 +499,7 @@
     anywhere = pl.BlockSpec(memory_space=pl.ANY)
     vmem = pl.BlockSpec(memory_space=pltpu.VMEM)
     attended, key_grad, value_grad = pl.pallas_call(
-        functools.partial(kernel, (nc, nh, hpd, T, R, S, D)),
+        functools.partial(kernel, (nc, nx, nh, hpd, T, R, S, D)),
         out_shape=(
             jax.ShapeDtypeStruct((heads_all, R, D), bf),
             jax.ShapeDtypeStruct((heads_all, T, D), f32),
@@ -395,10 +515,12 @@
             pltpu.VMEM((hpd, LANES, D), bf),
             pltpu.VMEM((hpd, LANES, D), bf),
             pltpu.VMEM((ny, hpd, 2, 1, R), jnp.int32),
-            pltpu.VMEM((ny, hpd, nc, S, 2 * D), bf),
+            pltpu.VMEM((ny, hpd, nc, S, D), bf),
+            pltpu.VMEM((ny, hpd, nc, S, D), bf),
             pltpu.VMEM((ny, hpd, 2, R, D), bf),
             pltpu.VMEM((ny, hpd, nc, S, 2 * D), bf),
-            pltpu.VMEM((nc, ny, hpd, S, 2 * D), bf),
+            pltpu.VMEM((ny, hpd, nc, S, 2 * D), bf),
+            pltpu.VMEM((nc, hpd, S, 2 * D), bf),
             pltpu.VMEM((hpd, S, 2 * D), f32),
             pltpu.VMEM((nh, hpd, T, 2 * D), bf),
             pltpu.VMEM((hpd, EDGE, 2 * D), bf),
@@ -406,8 +528,10 @@
             pltpu.VMEM((nh, hpd, EDGE, 2 * D), bf),
             dma((ny,)), dma((ny,)), dma((ny,)), dma((ny,)), dma((3 + 2 * ny,)),
             dma((nh, 2)), dma((nh, 2)), dma((nh, 2)), dma((2,)), dma((ny,)), dma((ny,)),
-            dma((nc,)), dma((nc,)), dma((ny, nc)), dma((ny, nc)), dma((ny,)), dma((ny,)),
-            dma((ny, nc)), dma((nc, ny)), dma((nh,)), dma((nh,)), dma(()), dma((nh,)),
+            dma((nz, 2)), dma((nz, 2)), dma((nx, nz)), dma((nx, nz)), dma((ny, nc)), dma((ny, nc)),
+            dma((ny, nz)), dma((ny, nz)), dma((nx, ny, nz)), dma((nx, ny, nz)), dma((ny,)), dma((ny,)),
+            dma((ny, hpd, nc)), dma((ny, hpd, nc)), dma((nc,)), dma((nc,)),
+            dma((nh,)), dma((nh,)), dma(()), dma((nh,)),
         ],
         compiler_params=pltpu.CompilerParams(
             collective_id=0, has_side_effects=True, vmem_limit_bytes=56 << 20

time: 66.3 us -> 61.8 us (0.932)
  Pallas kernels: 58.9 us -> 54.1 us
    pallas_call x1, Pallas kernels: 58.9 us -> 54.1 us  [per_device(): pl.pallas_call(functools.partial(kernel, (nc, nx, nh, hpd, T, R, S, D)),...]
where the time goes in v2:
time: 61.8 us; the launch traced here: 61.2 us
  Pallas kernels  54.1 us (88%)
  local copies, waits for them, and re-layouts  6.35 us (10%)
  between operations  0.68 us (1%)
    pallas_call x1, Pallas kernels, per_device(): pl.pallas_call(functools.partial(kernel, (nc, nx, nh, hpd, T, R, S, D)),...  54.1 us
    unnamed x9, local copies, waits for them, and re-layouts  4.77 us

profile of v2, /device:TPU:15, one launch (start us, length us, event | category | flops | bytes accessed | tf_op | source)
XLA Modules:
  0.0 61.2 jit_solution(11911108964379326719)
XLA Ops:
  0.6 0.0 copy-start.2
  0.6 0.7 %copy-done.2 = s32[2,2048]{1,0:T(2,128)S(1)} copy-done((s32[2,2048]{1,0:T(2,128)S(1)}, s32[2,2048]{1,0:T(2,128)}, u32[]{:S(2)}) %copy-start.2) | copy-done | bytes 16408
  1.4 0.6 reshape.29.id_ref
  2.0 0.1 reshape.30
  2.0 0.1 broadcast_in_dim.5
  2.2 0.2 broadcast_in_dim.6
  2.3 0.6 %copy.11 = s32[2,2,2,1,512]{4,3,2,0,1:T(1,128)} copy(s32[2,2,2,1,512]{4,2,1,0,3:T(2,128)S(1)} %broadcast_in_dim.6) | data formatting | bytes 32768 | tf_op jit(solution)/shard_map/broadcast_in_dim | solution.py:495
  3.0 54.1 %shard_map.76 = (bf16[8,512,128]{2,1,0:T(8,128)(2,1)}, f32[8,64,128]{2,1,0:T(8,128)}, f32[8,64,128]{2,1,0:T(8,128)}) custom-call(bf16[8,512,128]{2,1,0:T(8,128)(2,1)} %bitcast.8, bf16[8,512,128]{2,1,0:T(8,128)(2,1)} %bitcast.9, bf16[8,64,128]{2,1,0:T(8,128)(2,1)} %k_ref.1, bf16[8,64,128]{2,1,0:T(8,128)(2,1)} %v_ref.1, s32[2,1,384]{2,1,0:T(1,128)} %reshape.29.id_ref, ...), custom_call_target="tpu_custom_call" | custom-call | tf_op jit(solution)/shard_map/pallas_call | solution.py:501
  57.1 0.0 copy-start.1
  57.1 2.3 %copy.15 = bf16[8,64,8,128]{3,2,1,0:T(8,128)(2,1)} copy(bf16[8,64,8,128]{3,2,1,0:T(8,128)(2,1)} %bitcast.10) | data formatting | bytes 2097152
  59.4 0.0 copy-done.1
  59.4 0.0 copy-start
  59.4 0.7 %copy.16 = f32[8,64,128]{2,1,0:T(8,128)} copy(f32[8,64,128]{2,1,0:T(8,128)S(1)} %copy-done.1) | data formatting | bytes 524288
  60.1 0.3 copy-done
  60.5 0.7 %copy.17 = f32[8,64,128]{2,1,0:T(8,128)} copy(f32[8,64,128]{2,1,0:T(8,128)S(1)} %copy-done) | data formatting | bytes 524288
  (2 shorter events, 0.0 us)
Async XLA Ops:
  0.6 0.7 %copy-start.2 = (s32[2,2048]{1,0:T(2,128)S(1)}, s32[2,2048]{1,0:T(2,128)}, u32[]{:S(2)}) copy-start(s32[2,2048]{1,0:T(2,128)} %param.9) | copy-start | bytes 49156
  57.1 2.3 %copy-start.1 = (f32[8,64,128]{2,1,0:T(8,128)S(1)}, f32[8,64,128]{2,1,0:T(8,128)}, u32[]{:S(2)}) copy-start(f32[8,64,128]{2,1,0:T(8,128)} %get-tuple-element.13) | copy-start | bytes 786436
  59.4 1.0 %copy-start = (f32[8,64,128]{2,1,0:T(8,128)S(1)}, f32[8,64,128]{2,1,0:T(8,128)}, u32[]{:S(2)}) copy-start(f32[8,64,128]{2,1,0:T(8,128)} %get-tuple-element.14) | copy-start | bytes 786436

commit v3 on v2

--- a/solution.py
+++ b/solution.py
@@ -93,7 +93,7 @@
         )
 
     def thr_copy(to_y, frm_y):
-        return remote(thr_ref.at[to_y], thrb.at[frm_y], thr_s.at[to_y], thr_r.at[frm_y], ctx, to_y * 2 + c)
+        return remote(thr_ref.at[:, to_y], thrb.at[frm_y], thr_s.at[to_y], thr_r.at[frm_y], ctx, to_y * 2 + c)
 
     def swap_copy(yy, kv, core):
         src, dst, ss, sr = ((q_ref, qb, q_s, q_r), (g_ref, gb, g_s, g_r))[kv]
@@ -162,7 +162,7 @@
         pltpu.make_async_copy(heads(k_ref, j), tk.at[:, j], loc.at[0]),
         pltpu.make_async_copy(heads(v_ref, j), tv.at[:, j], loc.at[1]),
     ]
-    own_thr = pltpu.make_async_copy(thr_ref.at[y], thrb.at[y], loc.at[2])
+    own_thr = pltpu.make_async_copy(thr_ref.at[:, y], thrb.at[y], loc.at[2])
     for cp in own_tok:
         cp.start()
     own_thr.start()
@@ -196,7 +196,7 @@
         cp.wait()
 
     def hot(h):
-        rel = id_ref[h]
+        rel = id_ref[h:h + 1]
         main = lax.broadcasted_iota(jnp.int32, (S, TB), 0) == rel[:, :TB]
         edge = lax.broadcasted_iota(jnp.int32, (S, LANES), 0) == rel[:, TB:]
         main, edge = main.astype(jnp.float32), edge.astype(jnp.float32)
@@ -476,6 +476,12 @@
         tx_copy(ctx + 1, j).wait_send()
 
 
+def hand_over(a_ref, k_ref, v_ref, a_out, k_out, v_out):
+    a_out[...] = a_ref[...]
+    k_out[...] = k_ref[...]
+    v_out[...] = v_ref[...]
+
+
 def per_device(nc, nh, token_keys, token_values, queries, out_grad, slot_ids):
     heads_all, T, D = token_keys.shape
     group = queries.shape[2]
@@ -490,10 +496,9 @@
     ctx = lax.axis_index("ctx")
     padded = jnp.pad(slot_ids, ((0, 0), (0, LANES)), constant_values=context)
     window = lax.dynamic_slice_in_dim(padded, ctx * TB, TB + LANES, 1)
-    relative = (window - ctx * S).reshape(hpd, 1, TB + LANES)
+    relative = window - ctx * S
     seen_at = window[:, stride - 1:TB:stride]
     limit = jnp.repeat(seen_at.reshape(hpd, ny, 2, 1, R // group), group, axis=4)
-    limit = limit.transpose(1, 0, 2, 3, 4)
     bf, f32 = jnp.bfloat16, jnp.float32
     dma = pltpu.SemaphoreType.DMA
     anywhere = pl.BlockSpec(memory_space=pl.ANY)
@@ -540,6 +545,18 @@
         queries.reshape(heads_all, R, D), out_grad.reshape(heads_all, R, D),
         token_keys, token_values, relative, limit,
     )
+    results = (attended, key_grad, value_grad)
+
+    def by_head(r):
+        return pl.BlockSpec((heads_all // 2,) + r.shape[1:], lambda i: (i, 0, 0))
+
+    attended, key_grad, value_grad = pl.pallas_call(
+        hand_over,
+        out_shape=tuple(jax.ShapeDtypeStruct(r.shape, r.dtype) for r in results),
+        grid=(2,),
+        in_specs=[by_head(r) for r in results],
+        out_specs=tuple(by_head(r) for r in results),
+    )(*results)
     return attended.reshape(queries.shape), key_grad, value_grad
 
 

time: 61.8 us -> 60.1 us (0.972)
  local copies, waits for them, and re-layouts: 6.35 us -> 1.7 us
  Pallas kernels: 54.1 us -> 56.5 us
    unnamed x9 -> x2, local copies, waits for them, and re-layouts: 4.77 us -> 0.7 us
    pallas_call x0 -> x1, Pallas kernels: none -> 2.33 us  [per_device(): pl.pallas_call(hand_over, out_shape=tuple((jax.ShapeDtypeStruct(r.shape,...]
where the time goes in v3:
time: 60.1 us; the launch traced here: 59.4 us
  Pallas kernels  56.5 us (94%)
  local copies, waits for them, and re-layouts  1.7 us (3%)
  between operations  0.66 us (1%)
    pallas_call x1, Pallas kernels, per_device(): pl.pallas_call(functools.partial(kernel, (nc, nx, nh, hpd, T, R, S, D)),...  54.2 us
    pallas_call x1, Pallas kernels, per_device(): pl.pallas_call(hand_over, out_shape=tuple((jax.ShapeDtypeStruct(r.shape,...  2.33 us

profile of v3, /device:TPU:15, one launch (start us, length us, event | category | flops | bytes accessed | tf_op | source)
XLA Modules:
  0.0 59.4 jit_solution(17464915688835085330)
XLA Ops:
  0.6 0.0 copy-start
  0.6 0.7 %copy-done = s32[2,2048]{1,0:T(2,128)S(1)} copy-done((s32[2,2048]{1,0:T(2,128)S(1)}, s32[2,2048]{1,0:T(2,128)}, u32[]{:S(2)}) %copy-start) | copy-done | bytes 16408
  1.4 0.6 fusion.id_ref
  1.9 0.1 reshape.26
  2.0 0.1 broadcast_in_dim.5
  2.2 0.8 %broadcast_in_dim.7.thr_ref = s32[2,2,2,1,512]{4,3,2,1,0:T(1,128)} reshape(s32[2,2,2,64,8]{4,3,2,1,0:T(8,128)S(1)} %broadcast_in_dim.5) | data formatting | bytes 32768 | tf_op jit(solution)/shard_map/broadcast_in_dim | solution.py:501
  2.9 54.2 %shard_map.76 = (bf16[8,512,128]{2,1,0:T(8,128)(2,1)}, f32[8,64,128]{2,1,0:T(8,128)}, f32[8,64,128]{2,1,0:T(8,128)}) custom-call(bf16[8,512,128]{2,1,0:T(8,128)(2,1)} %bitcast.5, bf16[8,512,128]{2,1,0:T(8,128)(2,1)} %bitcast.6, bf16[8,64,128]{2,1,0:T(8,128)(2,1)} %k_ref.1, bf16[8,64,128]{2,1,0:T(8,128)(2,1)} %v_ref.1, s32[2,384]{1,0:T(2,128)} %fusion.id_ref, ...), custom_call_target="tpu_custom_call" | custom-call | tf_op jit(solution)/shard_map/pallas_call | solution.py:506
  57.1 2.3 %shard_map.77 = (bf16[8,512,128]{2,1,0:T(8,128)(2,1)}, f32[8,64,128]{2,1,0:T(8,128)}, f32[8,64,128]{2,1,0:T(8,128)}) custom-call(bf16[8,512,128]{2,1,0:T(8,128)(2,1)} %get-tuple-element.9.a_ref, f32[8,64,128]{2,1,0:T(8,128)} %get-tuple-element.10.k_ref, f32[8,64,128]{2,1,0:T(8,128)} %get-tuple-element.11.v_ref), custom_call_target="tpu_custom_call" | custom-call | tf_op jit(solution)/shard_map/pallas_call | solution.py:553
  (1 shorter events, 0.0 us)
Async XLA Ops:
  0.6 0.7 %copy-start = (s32[2,2048]{1,0:T(2,128)S(1)}, s32[2,2048]{1,0:T(2,128)}, u32[]{:S(2)}) copy-start(s32[2,2048]{1,0:T(2,128)} %param.9) | copy-start | bytes 49156
